TPU v7x, 512 devices: a whole 4x8x8 slice. The times are simulated.
512 devices in a mesh: req: 64 (over z_lo, x, y), tp: 8 (over z_hi, core).
Axes of the slice: x: 4, y: 8, z: 8 (z_hi: 4, z_lo: 2; z = z_hi * 2 + z_lo), core: 2. Of those that a mesh axis runs over, the one named last changes fastest.
Arguments:
- q_proj: bfloat16 [64, 128, 3072], P('req', None, 'tp'), may hold values from -24 to 24, as said below
- kv_proj: bfloat16 [64, 128, 2, 1024], P('req', None, None, 'tp'), may hold values from -6 to 6
- q_bias: bfloat16 [3072], P('tp'), may hold values from -3 to 3
- kv_bias: bfloat16 [2, 1024], P(None, 'tp'), may hold values from -3 to 3
- prefix_kv: bfloat16 [64, 1024, 2, 1024], P('req', None, None, 'tp'), may hold values from -24 to 24, as said below
- lengths: int32 [64], P('req'), may hold values from 1 to 128, 4096 in all
- group_of: int32 [64], P('req'), may hold values from 0 to 2
- owner: int32 [3], replicated, may hold values from 0 to 63
- positions: int32 [64, 128], P('req'), may hold values from 1024 to 1278, as said below
- residual: bfloat16 [64, 128, 5120], P('req', None, 'tp'), may hold values from -6 to 6
- out_weight: bfloat16 [3072, 5120], P(None, 'tp'), may hold values from -0.109375 to 0.109375
Outputs:
- hidden: bfloat16 [64, 128, 5120], P('req', None, 'tp')
Inputs may be any that keep to these rules, and one draw needn't show every extreme that they name: `q_proj`: projected queries; entries stay within the stated bounds. `prefix_kv`: cached keys are already rotated at prefix positions 0 to 1023. Each request's positions are a start of 1024 or more plus the slot index.
All inputs are finite; a program needn't handle non-finite values. No bound on the sum of `lengths` on one device may be relied on, other than what follows from the above.
Results may differ from a plain program's by a relative error of at most 0.006.
Values may be sent and summed in bfloat16 or wider, within the bound.
No kernel may reach another device: no remote copies, remote signals or barrier semaphores. Data moves between devices by JAX's collectives and lax.ppermute only.
A program may use at most 128 MiB of HBM per device.

v0:
```python
import math
import jax
import jax.numpy as jnp
from jax import lax
from jax.sharding import PartitionSpec as P

HD = 128


def rotate(vectors, places):
    half = HD // 2
    index = jnp.arange(half).astype(jnp.float32)
    freqs = jnp.exp(index * (-2.0 / HD) * math.log(1000000.0))
    angles = places.astype(jnp.float32)[:, None] * freqs[None, :]
    cosine = jnp.concatenate([jnp.cos(angles), jnp.cos(angles)], axis=-1)[:, None, :]
    sine = jnp.concatenate([jnp.sin(angles), jnp.sin(angles)], axis=-1)[:, None, :]
    turned = jnp.concatenate([-vectors[..., half:], vectors[..., :half]], axis=-1)
    return vectors * cosine + turned * sine


def fetch_prefix(slab, group, owner):
    columns = lax.axis_size("req")
    piece = slab.shape[0] // columns
    pieces = slab.reshape(columns, piece, 2, HD)
    tag = jnp.broadcast_to(group.astype(slab.dtype), (columns, 1, 2, HD))
    spread = lax.all_to_all(jnp.concatenate([pieces, tag], axis=1), "req", 0, 0, tiled=True)
    groups = spread[:, piece, 0, 0].astype(jnp.int32)
    owned = [
        jnp.swapaxes(lax.dynamic_index_in_dim(spread, owner[g], 0, keepdims=False)[:piece], 0, 1)
        for g in range(owner.shape[0])
    ]
    outgoing = jnp.broadcast_to(owned[0], (columns, 2, piece, HD))
    for g in range(1, owner.shape[0]):
        outgoing = jnp.where((groups == g)[:, None, None, None], owned[g][None], outgoing)
    return lax.all_to_all(outgoing, "req", 0, 0, tiled=True)


def attend_rows(queries, all_keys, all_vals, length, prefix_len):
    count = queries.shape[0]
    slots = jnp.arange(count)
    causal = slots[None, :] <= slots[:, None]
    allowed = jnp.concatenate([jnp.ones((count, prefix_len), dtype=bool), causal], axis=1)
    scores = jnp.einsum("rhd,kd->hrk", queries, all_keys, preferred_element_type=jnp.float32) * (
        1.0 / math.sqrt(HD)
    )
    scores = jnp.where(allowed[None], scores, -1e30)
    top = jnp.max(scores, axis=-1, keepdims=True)
    weights = jnp.where(allowed[None], jnp.exp(scores - top), 0.0)
    total = jnp.sum(weights, axis=-1)
    rounded = weights.astype(jnp.bfloat16)
    mixed = jnp.einsum("hrk,kd->rhd", rounded, all_vals, preferred_element_type=jnp.float32)
    mixed = mixed / jnp.transpose(total)[:, :, None]
    mixed = jnp.where((slots < length)[:, None, None], mixed, 0.0)
    return mixed.astype(jnp.bfloat16)


def body(
    q_proj,
    kv_proj,
    q_bias,
    kv_bias,
    prefix_kv,
    lengths,
    group_of,
    owner,
    positions,
    residual,
    out_weight,
):
    cap = q_proj.shape[1]
    prefix_len = prefix_kv.shape[1]
    length = lengths[0]
    places = positions[0]
    slab = fetch_prefix(prefix_kv[0], group_of[0], owner)
    queries = q_proj[0].astype(jnp.float32).reshape(cap, -1, HD) + q_bias.astype(
        jnp.float32
    ).reshape(-1, HD)
    queries = rotate(queries, places).astype(jnp.bfloat16)
    pairs = kv_proj[0].astype(jnp.float32) + kv_bias.astype(jnp.float32)
    keys = rotate(pairs[:, 0][:, None, :], places)[:, 0].astype(jnp.bfloat16)
    vals = pairs[:, 1].astype(jnp.bfloat16)
    all_keys = jnp.concatenate([slab[:, 0].reshape(prefix_len, HD), keys], axis=0)
    all_vals = jnp.concatenate([slab[:, 1].reshape(prefix_len, HD), vals], axis=0)
    attended = attend_rows(queries, all_keys, all_vals, length, prefix_len)
    attended = attended.reshape(cap, -1)
    whole_heads = lax.all_gather(attended, "tp", axis=1, tiled=True)
    projected = jnp.dot(whole_heads, out_weight, preferred_element_type=jnp.float32)
    hidden = (residual[0].astype(jnp.float32) + projected).astype(jnp.bfloat16)
    return hidden[None]


def solution(mesh):
    in_specs = (
        P("req", None, "tp"),
        P("req", None, None, "tp"),
        P("tp"),
        P(None, "tp"),
        P("req", None, None, "tp"),
        P("req"),
        P("req"),
        P(),
        P("req", None),
        P("req", None, "tp"),
        P(None, "tp"),
    )
    out_specs = P("req", None, "tp")
    return jax.shard_map(body, mesh=mesh, in_specs=in_specs, out_specs=out_specs, check_vma=False)
```

profile of v0, /device:TPU:1, one launch (start us, length us, event | category | flops | bytes accessed | tf_op | source)
XLA Modules:
  0.0 89.6 jit_solution(15967355962080478842)
XLA Ops:
  0.0 1.1 %copy.38 = bf16[1,1024,2,128]{3,1,2,0:T(8,128)(2,1)S(1)} copy(bf16[1,1024,2,128]{3,2,1,0:T(2,128)(2,1)} %param.15) | data formatting | bytes 1048576 | tf_op args[4]
  1.1 0.0 copy-start.3
  1.1 0.0 copy-start.5
  1.1 0.0 copy-start.2
  1.1 0.0 copy-start.1
  1.2 0.0 copy-start.6
  1.2 0.5 copy.61
  2.4 0.0 copy-start.4
  2.4 1.2 %concatenate.45.clone = bf16[64,17,2,128]{3,2,1,0:T(2,128)(2,1)} pad(bf16[64,16,2,128]{3,2,1,0:T(2,128)(2,1)S(1)} %copy.61, bf16[]{:T(256)} %bitcast.3), padding=0_0x0_1x0_0x0_0 | pad | bytes 1081346 | tf_op jit(solution)/shard_map/concatenate | solution.py:26
  3.6 12.9 %all-to-all-start = ((bf16[64,17,2,128]{3,2,1,0:T(2,128)(2,1)}), bf16[64,17,2,128]{3,2,1,0:T(2,128)(2,1)S(1)}, u32[]{:S(2)}, u32[]{:S(2)}) async-start(bf16[64,17,2,128]{3,2,1,0:T(2,128)(2,1)} %concatenate.45.clone), calls=%async_computation | async-start | bytes 1114112 | tf_op jit(solution)/shard_map/all_to_all | solution.py:26
  16.5 0.0 copy-done.3
  16.5 0.6 fusion.32
  21.0 0.0 copy-done.5
  21.0 0.0 copy-done.2
  21.1 0.1 copy.46
  21.2 0.0 copy-done.1
  21.2 0.1 copy.47
  21.3 0.0 copy-done.6
  21.3 0.3 fusion.22
  21.6 0.1 pad_maximum_fusion
  21.7 0.1 copy.49
  21.8 0.1 copy.48
  24.6 0.0 copy-done.4
  24.6 0.1 slice_negate_fusion.1
  24.7 9.1 %all-to-all-done = bf16[64,17,2,128]{3,2,1,0:T(2,128)(2,1)S(1)} async-done(((bf16[64,17,2,128]{3,2,1,0:T(2,128)(2,1)}), bf16[64,17,2,128]{3,2,1,0:T(2,128)(2,1)S(1)}, u32[]{:S(2)}, u32[]{:S(2)}) %all-to-all-start) | async-done | bytes 557088 | tf_op jit(solution)/shard_map/all_to_all | solution.py:26
  33.8 2.4 %compare_reduce_fusion.1 = (pred[64]{0:T(512)(128)(4,1)S(1)}, pred[64]{0:T(512)(128)(4,1)S(1)}) fusion(bf16[64,17,2,128]{3,2,1,0:T(2,128)(2,1)S(1)} %all-to-all-done), kind=kLoop, calls=%fused_computation.28 | loop fusion | flops 192 | bytes 256 | tf_op jit(solution)/shard_map/eq | solution.py:34
  36.2 1.0 %select_select_fusion = bf16[64,2,16,128]{3,2,1,0:T(8,128)(2,1)} fusion(pred[64]{0:T(512)(128)(4,1)S(1)} %get-tuple-element.6, pred[64]{0:T(512)(128)(4,1)S(1)} %get-tuple-element.5, bf16[2,16,128]{2,1,0:T(8,128)(2,1)S(1)} %get-tuple-element.22, bf16[2,16,128]{2,1,0:T(8,128)(2,1)S(1)} %get-tuple-element.23, bf16[2,16,128]{2,1,0:T(8,128)(2,1)S(1)} %bitcast.89), kind=kLoop, calls=%fused_computation.15 | loop fusion | flops 524288 | bytes 548992 | tf_op jit(solution)/shard_map/jit(_where)/select_n | solution.py:34
  37.2 6.3 %all-to-all-start.1 = ((bf16[64,2,16,128]{3,2,1,0:T(8,128)(2,1)}), bf16[64,2,16,128]{3,2,1,0:T(8,128)(2,1)S(1)}, u32[]{:S(2)}, u32[]{:S(2)}) async-start(bf16[64,2,16,128]{3,2,1,0:T(8,128)(2,1)} %select_select_fusion), calls=%async_computation.1 | async-start | bytes 1048576 | tf_op jit(solution)/shard_map/all_to_all | solution.py:35
  43.5 0.1 fusion.21
  43.6 0.1 convert_add_fusion
  43.8 0.1 fusion.17
  43.9 15.3 %all-to-all-done.1 = bf16[64,2,16,128]{3,2,1,0:T(8,128)(2,1)S(1)} async-done(((bf16[64,2,16,128]{3,2,1,0:T(8,128)(2,1)}), bf16[64,2,16,128]{3,2,1,0:T(8,128)(2,1)S(1)}, u32[]{:S(2)}, u32[]{:S(2)}) %all-to-all-start.1) | async-done | bytes 524320 | tf_op jit(solution)/shard_map/all_to_all | solution.py:35
  59.2 0.4 fusion.3
  59.7 0.9 %fusion.33 = f32[3,128]{1,0:T(4,128)S(1)} fusion(bf16[128,3,128]{0,2,1:T(8,128)(2,1)S(1)} %fusion.17, pred[128,1152]{0,1:T(8,128)(4,1)S(1)} %concatenate.47, bf16[128,128]{1,0:T(8,128)(2,1)S(1)} %fusion.21, bf16[1024,128]{1,0:T(8,128)(2,1)S(1)} %bitcast.84), kind=kOutput, calls=%fused_computation.64 | convolution fusion | flops 116049024 | bytes 542208 | tf_op jit(solution)/shard_map/sub | solution.py:48
  60.6 0.1 copy.45
  60.7 0.0 copy-start
  60.7 0.6 fusion.10
  61.4 24.6 %all_gather.3 = bf16[128,3072]{0,1:T(8,128)(2,1)S(1)} all-gather(bf16[128,384]{0,1:T(8,128)(2,1)S(1)} %bitcast.88), channel_id=1, replica_groups=mesh['req'=64,'tp'=8] {'tp'}, dimensions={1}, use_global_device_ids=true | all-gather | bytes 884736 | tf_op jit(solution)/shard_map/all_gather | solution.py:86
  85.9 0.0 copy-done
  85.9 3.6 %fusion.9 = bf16[1,128,640]{2,1,0:T(8,128)(2,1)} fusion(bf16[128,3072]{0,1:T(8,128)(2,1)S(1)} %all_gather.3, bf16[3072,640]{1,0:T(8,128)(2,1)} %param.21, bf16[1,128,640]{2,1,0:T(8,128)(2,1)S(1)} %copy-done), kind=kOutput, calls=%fused_computation.12 | convolution fusion | flops 503562240 | bytes 5046272 | tf_op jit(solution)/shard_map/dot_general | solution.py:87
  (14 shorter events, 0.2 us)
Async XLA Ops:
  1.1 15.4 %copy-start.3 = (s32[3]{0:T(128)S(1)}, s32[3]{0:T(128)}, u32[]{:S(2)}) copy-start(s32[3]{0:T(128)} %param.18) | copy-start | bytes 40
  1.1 19.9 %copy-start.5 = (bf16[2,128]{1,0:T(2,128)(2,1)S(1)}, bf16[2,128]{1,0:T(2,128)(2,1)}, u32[]{:S(2)}) copy-start(bf16[2,128]{1,0:T(2,128)(2,1)} %param.14) | copy-start | bytes 1540
  1.1 19.9 %copy-start.2 = (bf16[1,128,2,128]{3,2,1,0:T(2,128)(2,1)S(1)}, bf16[1,128,2,128]{3,2,1,0:T(2,128)(2,1)}, u32[]{:S(2)}) copy-start(bf16[1,128,2,128]{3,2,1,0:T(2,128)(2,1)} %param.12) | copy-start | bytes 196612
  1.1 20.0 %copy-start.1 = (bf16[1,128,384]{2,1,0:T(8,128)(2,1)S(1)}, bf16[1,128,384]{2,1,0:T(8,128)(2,1)}, u32[]{:S(2)}) copy-start(bf16[1,128,384]{2,1,0:T(8,128)(2,1)} %param.11) | copy-start | bytes 294916
  1.2 20.1 %copy-start.6 = (s32[1,128]{1,0:T(1,128)S(1)}, s32[1,128]{1,0:T(1,128)}, u32[]{:S(2)}) copy-start(s32[1,128]{1,0:T(1,128)} %param.19) | copy-start | bytes 1540
  2.4 22.2 %copy-start.4 = (bf16[384]{0:T(512)(128)(2,1)S(1)}, bf16[384]{0:T(512)(128)(2,1)}, u32[]{:S(2)}) copy-start(bf16[384]{0:T(512)(128)(2,1)} %param.13) | copy-start | bytes 2308
  3.6 30.2 %all-to-all-start = ((bf16[64,17,2,128]{3,2,1,0:T(2,128)(2,1)}), bf16[64,17,2,128]{3,2,1,0:T(2,128)(2,1)S(1)}, u32[]{:S(2)}, u32[]{:S(2)}) async-start(bf16[64,17,2,128]{3,2,1,0:T(2,128)(2,1)} %concatenate.45.clone), calls=%async_computation | async-start | bytes 1114112 | tf_op jit(solution)/shard_map/all_to_all | solution.py:26
  37.2 22.0 %all-to-all-start.1 = ((bf16[64,2,16,128]{3,2,1,0:T(8,128)(2,1)}), bf16[64,2,16,128]{3,2,1,0:T(8,128)(2,1)S(1)}, u32[]{:S(2)}, u32[]{:S(2)}) async-start(bf16[64,2,16,128]{3,2,1,0:T(8,128)(2,1)} %select_select_fusion), calls=%async_computation.1 | async-start | bytes 1048576 | tf_op jit(solution)/shard_map/all_to_all | solution.py:35
  60.7 25.2 %copy-start = (bf16[1,128,640]{2,1,0:T(8,128)(2,1)S(1)}, bf16[1,128,640]{2,1,0:T(8,128)(2,1)}, u32[]{:S(2)}) copy-start(bf16[1,128,640]{2,1,0:T(8,128)(2,1)} %param.20) | copy-start | bytes 491524
where the time goes:
time: 90 us; the launch traced here: 89.6 us
  blocking collectives  24.6 us (27%)
  waiting for transfers between devices  24.4 us (27%)
  starting transfers between devices  19.2 us (21%)
  between operations  7.34 us (8%)
  matrix products  5.58 us (6%)
  other arithmetic  4.3 us (5%)
  local copies, waits for them, and re-layouts  4.2 us (5%)
    all_gather x1, blocking collectives, body(): whole_heads = lax.all_gather(attended, 'tp', axis=1, tiled=True)  24.6 us
    all_to_all x1, waiting for transfers between devices, fetch_prefix(): return lax.all_to_all(outgoing, 'req', 0, 0, tiled=True)  15.3 us
    all_to_all x1, starting transfers between devices, fetch_prefix(): lax.all_to_all(jnp.concatenate([pieces, tag], axis=1), 'req', 0, 0, tiled...  12.9 us
    all_to_all x1, waiting for transfers between devices, fetch_prefix(): lax.all_to_all(jnp.concatenate([pieces, tag], axis=1), 'req', 0, 0, tiled...  9.09 us
    all_to_all x1, starting transfers between devices, fetch_prefix(): return lax.all_to_all(outgoing, 'req', 0, 0, tiled=True)  6.25 us
    dot_general x1, matrix products, body(): jnp.dot(whole_heads, out_weight, preferred_element_type=jnp.float32)  3.62 us
    eq x1, other arithmetic, fetch_prefix(): groups == g  2.39 us
    unnamed x18, local copies, waits for them, and re-layouts  1.82 us
  transfers between devices with their start and end apart: 2, of which 2 were waited for; matrix products, arithmetic and copies ran while one was open for 2% of the time, Pallas kernels for 0%

commit v1 on v0

--- a/solution.py
+++ b/solution.py
@@ -83,7 +83,9 @@
     all_vals = jnp.concatenate([slab[:, 1].reshape(prefix_len, HD), vals], axis=0)
     attended = attend_rows(queries, all_keys, all_vals, length, prefix_len)
     attended = attended.reshape(cap, -1)
-    whole_heads = lax.all_gather(attended, "tp", axis=1, tiled=True)
+    whole_heads = jnp.concatenate(
+        lax.all_to_all(jnp.stack([attended] * lax.axis_size("tp")), "tp", 0, 0), axis=1
+    )
     projected = jnp.dot(whole_heads, out_weight, preferred_element_type=jnp.float32)
     hidden = (residual[0].astype(jnp.float32) + projected).astype(jnp.bfloat16)
     return hidden[None]

time: 90 us -> 100 us (1.11)
  the two profiles are of different devices: /device:TPU:1 before, /device:TPU:2 now
where the time goes in v1:
time: 100 us; the launch traced here: 99.9 us
  blocking collectives  33.2 us (33%)
  waiting for transfers between devices  26.8 us (27%)
  starting transfers between devices  18.4 us (18%)
  between operations  7.35 us (7%)
  matrix products  5.57 us (6%)
  local copies, waits for them, and re-layouts  4.3 us (4%)
  other arithmetic  4.3 us (4%)
    all_to_all x1, blocking collectives, body(): lax.all_to_all(jnp.stack([attended] * lax.axis_size('tp')), 'tp', 0, 0)  33.2 us
    all_to_all x1, waiting for transfers between devices, fetch_prefix(): return lax.all_to_all(outgoing, 'req', 0, 0, tiled=True)  16.4 us
    all_to_all x1, starting transfers between devices, fetch_prefix(): lax.all_to_all(jnp.concatenate([pieces, tag], axis=1), 'req', 0, 0, tiled...  12.5 us
    all_to_all x1, waiting for transfers between devices, fetch_prefix(): lax.all_to_all(jnp.concatenate([pieces, tag], axis=1), 'req', 0, 0, tiled...  10.3 us
    all_to_all x1, starting transfers between devices, fetch_prefix(): return lax.all_to_all(outgoing, 'req', 0, 0, tiled=True)  5.96 us
    dot_general x1, matrix products, body(): jnp.dot(whole_heads, out_weight, preferred_element_type=jnp.float32)  3.62 us
    eq x1, other arithmetic, fetch_prefix(): groups == g  2.39 us
  transfers between devices with their start and end apart: 2, of which 2 were waited for; matrix products, arithmetic and copies ran while one was open for 2% of the time, Pallas kernels for 0%

profile of v1, /device:TPU:2, one launch (start us, length us, event | category | flops | bytes accessed | tf_op | source)
XLA Modules:
  0.0 99.9 jit_solution(3016820370294271889)
XLA Ops:
  0.0 1.1 %copy.39 = bf16[1,1024,2,128]{3,1,2,0:T(8,128)(2,1)S(1)} copy(bf16[1,1024,2,128]{3,2,1,0:T(2,128)(2,1)} %param.15) | data formatting | bytes 1048576 | tf_op args[4]
  1.1 0.0 copy-start.3
  1.1 0.0 copy-start.5
  1.1 0.0 copy-start.2
  1.1 0.0 copy-start.1
  1.2 0.0 copy-start.6
  1.2 0.5 copy.62
  2.4 0.0 copy-start.4
  2.4 1.2 %concatenate.45.clone = bf16[64,17,2,128]{3,2,1,0:T(2,128)(2,1)} pad(bf16[64,16,2,128]{3,2,1,0:T(2,128)(2,1)S(1)} %copy.62, bf16[]{:T(256)} %bitcast.3), padding=0_0x0_1x0_0x0_0 | pad | bytes 1081346 | tf_op jit(solution)/shard_map/concatenate | solution.py:26
  3.6 12.5 %all-to-all-start = ((bf16[64,17,2,128]{3,2,1,0:T(2,128)(2,1)}), bf16[64,17,2,128]{3,2,1,0:T(2,128)(2,1)S(1)}, u32[]{:S(2)}, u32[]{:S(2)}) async-start(bf16[64,17,2,128]{3,2,1,0:T(2,128)(2,1)} %concatenate.45.clone), calls=%async_computation | async-start | bytes 1114112 | tf_op jit(solution)/shard_map/all_to_all | solution.py:26
  16.1 0.0 copy-done.3
  16.1 0.6 fusion.32
  20.5 0.0 copy-done.5
  20.5 0.0 copy-done.2
  20.6 0.1 copy.47
  20.7 0.0 copy-done.1
  20.7 0.1 copy.48
  20.8 0.0 copy-done.6
  20.9 0.3 fusion.22
  21.2 0.1 pad_maximum_fusion
  21.3 0.1 copy.50
  21.4 0.1 copy.49
  24.1 0.0 copy-done.4
  24.1 0.1 slice_negate_fusion.1
  24.2 10.3 %all-to-all-done = bf16[64,17,2,128]{3,2,1,0:T(2,128)(2,1)S(1)} async-done(((bf16[64,17,2,128]{3,2,1,0:T(2,128)(2,1)}), bf16[64,17,2,128]{3,2,1,0:T(2,128)(2,1)S(1)}, u32[]{:S(2)}, u32[]{:S(2)}) %all-to-all-start) | async-done | bytes 557088 | tf_op jit(solution)/shard_map/all_to_all | solution.py:26
  34.6 2.4 %compare_reduce_fusion.1 = (pred[64]{0:T(512)(128)(4,1)S(1)}, pred[64]{0:T(512)(128)(4,1)S(1)}) fusion(bf16[64,17,2,128]{3,2,1,0:T(2,128)(2,1)S(1)} %all-to-all-done), kind=kLoop, calls=%fused_computation.28 | loop fusion | flops 192 | bytes 256 | tf_op jit(solution)/shard_map/eq | solution.py:34
  37.0 1.0 %select_select_fusion = bf16[64,2,16,128]{3,2,1,0:T(8,128)(2,1)} fusion(pred[64]{0:T(512)(128)(4,1)S(1)} %get-tuple-element.6, pred[64]{0:T(512)(128)(4,1)S(1)} %get-tuple-element.5, bf16[2,16,128]{2,1,0:T(8,128)(2,1)S(1)} %get-tuple-element.22, bf16[2,16,128]{2,1,0:T(8,128)(2,1)S(1)} %get-tuple-element.23, bf16[2,16,128]{2,1,0:T(8,128)(2,1)S(1)} %bitcast.93), kind=kLoop, calls=%fused_computation.15 | loop fusion | flops 524288 | bytes 548992 | tf_op jit(solution)/shard_map/jit(_where)/select_n | solution.py:34
  38.0 6.0 %all-to-all-start.1 = ((bf16[64,2,16,128]{3,2,1,0:T(8,128)(2,1)}), bf16[64,2,16,128]{3,2,1,0:T(8,128)(2,1)S(1)}, u32[]{:S(2)}, u32[]{:S(2)}) async-start(bf16[64,2,16,128]{3,2,1,0:T(8,128)(2,1)} %select_select_fusion), calls=%async_computation.1 | async-start | bytes 1048576 | tf_op jit(solution)/shard_map/all_to_all | solution.py:35
  44.0 0.1 fusion.21
  44.1 0.1 convert_add_fusion
  44.2 0.1 fusion.17
  44.4 16.4 %all-to-all-done.1 = bf16[64,2,16,128]{3,2,1,0:T(8,128)(2,1)S(1)} async-done(((bf16[64,2,16,128]{3,2,1,0:T(8,128)(2,1)}), bf16[64,2,16,128]{3,2,1,0:T(8,128)(2,1)S(1)}, u32[]{:S(2)}, u32[]{:S(2)}) %all-to-all-start.1) | async-done | bytes 524320 | tf_op jit(solution)/shard_map/all_to_all | solution.py:35
  60.9 0.4 fusion.3
  61.3 0.9 fusion.33
  62.2 0.1 copy.46
  62.3 0.6 fusion.10
  63.0 0.0 copy-start
  63.0 0.1 stack.3
  63.1 33.2 %all_to_all.15 = bf16[8,128,384]{1,2,0:T(8,128)(2,1)S(1)} all-to-all(bf16[8,128,384]{1,2,0:T(8,128)(2,1)S(1)} %stack.3), channel_id=1, replica_groups=mesh['req'=64,'tp'=8] {'tp'}, dimensions={0} | all-to-all | bytes 1572864 | tf_op jit(solution)/shard_map/all_to_all | solution.py:87
  96.3 0.0 copy-done
  96.3 3.6 %fusion.9 = bf16[1,128,640]{2,1,0:T(8,128)(2,1)} fusion(bf16[128,3072]{0,1:T(8,128)(2,1)S(1)} %bitcast.85, bf16[3072,640]{1,0:T(8,128)(2,1)} %param.21, bf16[1,128,640]{2,1,0:T(8,128)(2,1)S(1)} %copy-done), kind=kOutput, calls=%fused_computation.12 | convolution fusion | flops 503562240 | bytes 5046272 | tf_op jit(solution)/shard_map/dot_general | solution.py:89
  (14 shorter events, 0.2 us)
Async XLA Ops:
  1.1 15.0 %copy-start.3 = (s32[3]{0:T(128)S(1)}, s32[3]{0:T(128)}, u32[]{:S(2)}) copy-start(s32[3]{0:T(128)} %param.18) | copy-start | bytes 40
  1.1 19.4 %copy-start.5 = (bf16[2,128]{1,0:T(2,128)(2,1)S(1)}, bf16[2,128]{1,0:T(2,128)(2,1)}, u32[]{:S(2)}) copy-start(bf16[2,128]{1,0:T(2,128)(2,1)} %param.14) | copy-start | bytes 1540
  1.1 19.4 %copy-start.2 = (bf16[1,128,2,128]{3,2,1,0:T(2,128)(2,1)S(1)}, bf16[1,128,2,128]{3,2,1,0:T(2,128)(2,1)}, u32[]{:S(2)}) copy-start(bf16[1,128,2,128]{3,2,1,0:T(2,128)(2,1)} %param.12) | copy-start | bytes 196612
  1.1 19.6 %copy-start.1 = (bf16[1,128,384]{2,1,0:T(8,128)(2,1)S(1)}, bf16[1,128,384]{2,1,0:T(8,128)(2,1)}, u32[]{:S(2)}) copy-start(bf16[1,128,384]{2,1,0:T(8,128)(2,1)} %param.11) | copy-start | bytes 294916
  1.2 19.7 %copy-start.6 = (s32[1,128]{1,0:T(1,128)S(1)}, s32[1,128]{1,0:T(1,128)}, u32[]{:S(2)}) copy-start(s32[1,128]{1,0:T(1,128)} %param.19) | copy-start | bytes 1540
  2.4 21.7 %copy-start.4 = (bf16[384]{0:T(512)(128)(2,1)S(1)}, bf16[384]{0:T(512)(128)(2,1)}, u32[]{:S(2)}) copy-start(bf16[384]{0:T(512)(128)(2,1)} %param.13) | copy-start | bytes 2308
  3.6 30.9 %all-to-all-start = ((bf16[64,17,2,128]{3,2,1,0:T(2,128)(2,1)}), bf16[64,17,2,128]{3,2,1,0:T(2,128)(2,1)S(1)}, u32[]{:S(2)}, u32[]{:S(2)}) async-start(bf16[64,17,2,128]{3,2,1,0:T(2,128)(2,1)} %concatenate.45.clone), calls=%async_computation | async-start | bytes 1114112 | tf_op jit(solution)/shard_map/all_to_all | solution.py:26
  38.0 22.8 %all-to-all-start.1 = ((bf16[64,2,16,128]{3,2,1,0:T(8,128)(2,1)}), bf16[64,2,16,128]{3,2,1,0:T(8,128)(2,1)S(1)}, u32[]{:S(2)}, u32[]{:S(2)}) async-start(bf16[64,2,16,128]{3,2,1,0:T(8,128)(2,1)} %select_select_fusion), calls=%async_computation.1 | async-start | bytes 1048576 | tf_op jit(solution)/shard_map/all_to_all | solution.py:35
  63.0 33.4 %copy-start = (bf16[1,128,640]{2,1,0:T(8,128)(2,1)S(1)}, bf16[1,128,640]{2,1,0:T(8,128)(2,1)}, u32[]{:S(2)}) copy-start(bf16[1,128,640]{2,1,0:T(8,128)(2,1)} %param.20) | copy-start | bytes 491524
